TPU v7x, 256 devices: a whole 4x4x8 slice. The times are simulated.
256 devices in a mesh: row: 8 (over x, core), col: 32 (over y, z).
Axes of the slice: x: 4, y: 4, z: 8, core: 2. Of those that a mesh axis runs over, the one named last changes fastest.
Arguments:
- hidden: bfloat16 [4096, 8192], P('row', 'col'), may hold values from -600 to 600
- norm_gain: float32 [8192], replicated, may hold values from 0.5 to 2
- wq: bfloat16 [8192, 8192], P('row', 'col'), may hold values from -1 to 1
- wk: bfloat16 [8192, 1024], P('row', 'col'), may hold values from -1 to 1
- wv: bfloat16 [8192, 1024], P('row', 'col'), may hold values from -0.0625 to 0.0625
- wo: bfloat16 [8192, 8192], P('row', 'col'), may hold values from -0.25 to 0.25
Outputs:
- attn_out: bfloat16 [4096, 8192], P('row', 'col')
All inputs are finite; a program needn't handle non-finite values.
Results may differ from a plain program's by a relative error of at most 0.011.
Values may be sent and summed in bfloat16 or wider, within the bound.
A program may use at most 64 MiB of HBM per device.

v0:
```python
import jax
import jax.numpy as jnp
from jax import lax
from jax.sharding import PartitionSpec as P

HD = 128


def partner(array, axis, distance):
    return lax.ppermute(array, axis, [(i, i ^ 1 << distance) for i in range(lax.axis_size(axis))])


def rotary(field, positions):
    half = field.shape[-1] // 2
    steps = jnp.arange(half).astype(jnp.float32)
    freqs = 10000.0 ** (-steps / half)
    angles = positions.astype(jnp.float32)[:, None] * freqs[None, :]
    cosine = jnp.cos(angles)[:, None, :]
    sine = jnp.sin(angles)[:, None, :]
    first = field[..., :half]
    second = field[..., half:]
    return jnp.concatenate(
        [first * cosine - second * sine, second * cosine + first * sine], axis=-1
    )


def order_pair(mine, other, col_index, bit, axis_dim):
    upper = col_index // 2**bit % 2 == 1
    lower_part = jnp.where(upper, other, mine)
    upper_part = jnp.where(upper, mine, other)
    return jnp.concatenate([lower_part, upper_part], axis=axis_dim)


def per_device(hidden, norm_gain, wq, wk, wv, wo):
    tok_rows = hidden.shape[0]
    panel = lax.all_gather(hidden, "col", axis=1, tiled=True)
    values_in = panel.astype(jnp.float32)
    meansq = jnp.mean(values_in * values_in, axis=1, keepdims=True)
    normed = (values_in * lax.rsqrt(meansq + 1e-05) * norm_gain).astype(jnp.bfloat16)
    kv_cols = wk.shape[1]
    group = max(1, HD // kv_cols)
    bits = group.bit_length() - 1
    col_index = lax.axis_index("col")
    stacked = jnp.stack((wk, wv), axis=1)
    for bit in range(bits):
        other = partner(stacked, "col", bit)
        stacked = order_pair(stacked, other, col_index, bit, 2)
    columns = normed
    query_part = jnp.dot(
        columns, lax.all_gather(wq, "row", axis=0, tiled=True), preferred_element_type=jnp.float32
    )
    pair_part = jnp.einsum(
        "ho,omr->hmr",
        columns,
        lax.all_gather(stacked, "row", axis=0, tiled=True),
        preferred_element_type=jnp.float32,
    )
    heads_here = wq.shape[1] // HD
    kv_here = pair_part.shape[2] // HD
    per_kv = heads_here // kv_here
    positions = lax.axis_index("row") * tok_rows + jnp.arange(tok_rows)
    queries = rotary(query_part.reshape(tok_rows, heads_here, HD), positions).astype(jnp.bfloat16)
    queries = queries.reshape(tok_rows, kv_here, per_kv, HD)
    keys = rotary(pair_part[:, 0].reshape(tok_rows, kv_here, HD), positions).astype(jnp.bfloat16)
    values = pair_part[:, 1].reshape(tok_rows, kv_here, HD).astype(jnp.bfloat16)
    scale = HD ** (-0.5)
    best = jnp.full((kv_here, per_kv, tok_rows), -1e30, jnp.float32)
    key_piece = lax.all_gather(keys, "row", axis=0, tiled=True)
    value_piece = lax.all_gather(values, "row", axis=0, tiled=True)
    count = key_piece.shape[0]
    scores = (
        jnp.einsum("tagd,nad->agtn", queries, key_piece, preferred_element_type=jnp.float32) * scale
    )
    key_pos = jnp.arange(count)
    visible = positions[:, None] >= key_pos[None, :]
    scores = jnp.where(visible, scores, -jnp.inf)
    fresh = jnp.maximum(best, jnp.max(scores, axis=3))
    probs = jnp.exp(scores - fresh[..., None])
    total = jnp.sum(probs, axis=3)
    update = jnp.einsum(
        "agtn,nad->agtd",
        probs.astype(jnp.bfloat16),
        value_piece,
        preferred_element_type=jnp.float32,
    )
    numer = update
    best, total, numer = (fresh, total, numer)
    heads = (
        (numer / total[..., None])
        .transpose(2, 0, 1, 3)
        .reshape(tok_rows, heads_here * HD)
        .astype(jnp.bfloat16)
    )
    head_panel = lax.all_gather(heads, "col", axis=1, tiled=True)
    columns = head_panel
    result = jnp.dot(
        columns, lax.all_gather(wo, "row", axis=0, tiled=True), preferred_element_type=jnp.float32
    )
    return result.astype(jnp.bfloat16)


def solution(mesh):
    in_specs = (
        P("row", "col"),
        P(),
        P("row", "col"),
        P("row", "col"),
        P("row", "col"),
        P("row", "col"),
    )
    out_specs = P("row", "col")
    return jax.shard_map(
        per_device, mesh=mesh, in_specs=in_specs, out_specs=out_specs, check_vma=False
    )
```

profile of v0, /device:TPU:1, one launch (start us, length us, event | category | flops | bytes accessed | tf_op | source)
XLA Modules:
  0.0 396.9 jit_solution(9538606364416327431)
XLA Ops:
  6.5 0.0 copy-start.1
  6.5 0.0 all-gather.8.cloned.1.call-start
  6.5 0.7 all-gather.8.cloned.1.call-update
  7.3 0.0 all-gather.10.cloned.1.call-start
  7.3 0.9 pad_maximum_fusion.2
  8.2 2.6 collective-permute-start
  10.7 2.4 collective-permute-done
  13.1 0.9 broadcast_select_fusion.3
  14.0 3.8 collective-permute-start.1
  17.9 11.3 %collective-permute-done.1 = bf16[1024,2,64]{0,2,1:T(8,128)(2,1)S(1)} collective-permute-done((bf16[1024,2,64]{0,2,1:T(8,128)(2,1)S(1)}, bf16[1024,2,64]{0,2,1:T(8,128)(2,1)S(1)}, u32[]{:S(2)}, u32[]{:S(2)}) %collective-permute-start.1) | collective-permute-done | bytes 262176 | tf_op jit(solution)/shard_map/ppermute | solution.py:10
  29.2 0.1 broadcast_select_fusion.1
  29.3 0.8 pad_maximum_fusion
  30.1 0.0 all-gather.10.cloned.1.call-update
  30.2 0.0 all-gather.14.cloned.1.call-start
  30.2 0.7 all-gather.14.cloned.1.call-update
  30.9 0.0 all-gather.12.cloned.1.call-start
  31.0 86.2 %all-gather.8.cloned.1.call-done = bf16[512,8192]{1,0:T(8,128)(2,1)} async-done(((bf16[512,256]{1,0:T(8,128)(2,1)}), bf16[512,8192]{1,0:T(8,128)(2,1)}) %all-gather.8.cloned.1.call-update) | async-done | bytes 8388624 | tf_op jit(solution)/shard_map/all_gather | solution.py:36
  117.1 5.1 %fusion = f32[512]{0:T(512)S(1)} fusion(bf16[512,8192]{1,0:T(8,128)(2,1)} %all-gather.8.cloned.1.call-done), kind=kLoop, calls=%fused_computation.2 | loop fusion | flops 12582400 | bytes 8390656 | tf_op jit(solution)/shard_map/reduce_sum | solution.py:38
  122.3 31.8 %all-gather.10.cloned.1.call-done = bf16[8192,2,128]{0,2,1:T(8,128)(2,1)} async-done(((bf16[1024,2,128]{0,2,1:T(8,128)(2,1)}), bf16[8192,2,128]{0,2,1:T(8,128)(2,1)}) %all-gather.10.cloned.1.call-update) | async-done | bytes 4194320 | tf_op jit(solution)/shard_map/all_gather | solution.py:55
  154.1 0.0 copy-done.1
  154.1 7.0 %fusion.12 = f32[512,256]{0,1:S(1)} fusion(bf16[8192,256]{0,1:T(8,128)(2,1)} %bitcast.61, bf16[512,8192]{1,0:T(8,128)(2,1)} %all-gather.8.cloned.1.call-done, f32[8192]{0:T(1024)S(1)} %copy-done.1, f32[512]{0:T(512)S(1)} %add_rsqrt_fusion), kind=kOutput, calls=%fused_computation.15 | convolution fusion | flops 2164260864 | bytes 13142016
  161.1 0.6 fusion.35
  161.7 0.7 pad_maximum_fusion.3
  162.4 0.0 all-gather.12.cloned.1.call-update
  162.4 0.0 all-gather.16.cloned.1.call-start
  162.4 0.7 slice.34
  163.1 0.0 all-gather.16.cloned.1.call-update
  163.1 0.0 all-gather.20.cloned.1.call-start
  163.2 0.5 all-gather.20.cloned.1.call-update
  163.7 0.2 all-gather.18.cloned.1.call-start
  163.9 1.8 multiply_cosine_fusion
  165.7 1.7 iota_compare_fusion
  167.5 23.2 %all-gather.14.cloned.1.call-done = bf16[8192,256]{1,0:T(8,128)(2,1)} async-done(((bf16[1024,256]{1,0:T(8,128)(2,1)}), bf16[8192,256]{1,0:T(8,128)(2,1)}) %all-gather.14.cloned.1.call-update) | async-done | bytes 4194320 | tf_op jit(solution)/shard_map/all_gather | solution.py:50
  190.6 7.6 %fusion.10 = f32[512,256]{0,1:T(8,128)S(1)} fusion(bf16[8192,256]{1,0:T(8,128)(2,1)} %all-gather.14.cloned.1.call-done, bf16[512,8192]{1,0:T(8,128)(2,1)} %all-gather.8.cloned.1.call-done, f32[8192]{0:T(1024)S(1)} %copy-done.1, f32[512]{0:T(512)S(1)} %add_rsqrt_fusion), kind=kOutput, calls=%fused_computation.14 | convolution fusion | flops 2164260864 | bytes 13142016 | tf_op jit(solution)/shard_map/dot_general | solution.py:49
  198.3 0.2 copy.14
  198.5 0.2 copy.15
  198.7 1.9 subtract_convert_fusion
  200.5 17.7 %all-gather.12.cloned.1.call-done = bf16[4096,1,128]{0,2,1:T(8,128)(2,1)} async-done(((bf16[512,1,128]{0,2,1:T(8,128)(2,1)}), bf16[4096,1,128]{0,2,1:T(8,128)(2,1)}) %all-gather.12.cloned.1.call-update) | async-done | bytes 1048592 | tf_op jit(solution)/shard_map/all_gather | solution.py:68
  218.2 5.1 %fusion.5 = (f32[2,512]{1,0:T(2,128)S(1)}, f32[4096,512,2]{1,0,2:T(8,128)S(1)}) fusion(pred[512,4096]{0,1:T(8,128)(4,1)S(1)} %iota_compare_fusion, bf16[512,2,64]{2,0,1:T(8,128)(2,1)} %get-tuple-element.6, bf16[512,2,64]{2,0,1:T(8,128)(2,1)S(1)} %get-tuple-element.5, bf16[4096,1,128]{0,2,1:T(8,128)(2,1)} %all-gather.12.cloned.1.call-done), kind=kOutput, calls=%fused_computation.9 | convolution fusion | flops 1086848000 | bytes 20189184 | tf_op jit(solution)/shard_map/tagd,nad->agtn/dot_general | solution.py:72
  223.3 0.0 copy-start
  223.3 5.7 %copy-done = f32[4096,512,2]{1,0,2:T(8,128)} copy-done((f32[4096,512,2]{1,0,2:T(8,128)}, f32[4096,512,2]{1,0,2:T(8,128)S(1)}, u32[]{:S(2)}) %copy-start) | copy-done | bytes 16777240
  229.0 4.2 %fusion.3 = f32[2,512]{1,0:T(2,128)S(1)} fusion(f32[4096,512,2]{1,0,2:T(8,128)S(1)} %get-tuple-element.18, f32[2,512]{1,0:T(2,128)S(1)} %broadcast_maximum_fusion, pred[512,4096]{0,1:T(8,128)(4,1)S(1)} %iota_compare_fusion), kind=kLoop, calls=%fused_computation.7 | loop fusion | flops 16776192 | bytes 18882560 | tf_op jit(solution)/shard_map/reduce_sum | solution.py:79
  233.2 12.6 %all-gather.16.cloned.1.call-done = bf16[4096,1,128]{0,2,1:T(8,128)(2,1)} async-done(((bf16[512,1,128]{0,2,1:T(8,128)(2,1)}), bf16[4096,1,128]{0,2,1:T(8,128)(2,1)}) %all-gather.16.cloned.1.call-update) | async-done | bytes 1048592 | tf_op jit(solution)/shard_map/all_gather | solution.py:69
  245.8 11.7 %fusion.22 = bf16[2,512,128]{1,2,0:T(8,128)(2,1)} fusion(f32[4096,512,2]{1,0,2:T(8,128)} %copy-done, f32[2,512]{1,0:T(2,128)S(1)} %broadcast_maximum_fusion, pred[512,4096]{0,1:T(8,128)(4,1)S(1)} %iota_compare_fusion, bf16[4096,1,128]{0,2,1:T(8,128)(2,1)} %all-gather.16.cloned.1.call-done, f32[2,512]{1,0:T(2,128)S(1)} %fusion.3), kind=kOutput, calls=%fused_computation.21 | convolution fusion | flops 1090781184 | bytes 20193280 | tf_op jit(solution)/shard_map/agtn,nad->agtd/dot_general | solution.py:80
  257.4 0.0 all-gather.18.cloned.1.call-update
  257.4 24.6 %all-gather.20.cloned.1.call-done = bf16[8192,256]{1,0:T(8,128)(2,1)} async-done(((bf16[1024,256]{1,0:T(8,128)(2,1)}), bf16[8192,256]{1,0:T(8,128)(2,1)}) %all-gather.20.cloned.1.call-update) | async-done | bytes 4194320 | tf_op jit(solution)/shard_map/all_gather | solution.py:97
  282.0 100.3 %all-gather.18.cloned.1.call-done = bf16[512,8192]{0,1:T(8,128)(2,1)} async-done(((bf16[512,256]{0,1:T(8,128)(2,1)}), bf16[512,8192]{0,1:T(8,128)(2,1)}) %all-gather.18.cloned.1.call-update) | async-done | bytes 8388624 | tf_op jit(solution)/shard_map/all_gather | solution.py:94
  382.4 7.7 %convolution_convert_fusion = bf16[512,256]{1,0:T(8,128)(2,1)} fusion(bf16[512,8192]{0,1:T(8,128)(2,1)} %all-gather.18.cloned.1.call-done, bf16[8192,256]{1,0:T(8,128)(2,1)} %all-gather.20.cloned.1.call-done), kind=kOutput, calls=%fused_computation.16 | convolution fusion | flops 2147614720 | bytes 12845056 | tf_op jit(solution)/shard_map/dot_general | solution.py:96
  (7 shorter events, 0.1 us)
Async XLA Ops:
  6.5 147.6 %copy-start.1 = (f32[8192]{0:T(1024)S(1)}, f32[8192]{0:T(1024)}, u32[]{:S(2)}) copy-start(f32[8192]{0:T(1024)} %param.7) | copy-start | bytes 98308
  6.5 110.6 %all-gather.8.cloned.1.call-start = ((), (), s32[]{:S(2)}) async-start(), calls=%async_computation | async-start | bytes 8650752 | tf_op jit(solution)/shard_map/all_gather | solution.py:36
  7.3 146.8 %all-gather.10.cloned.1.call-start = ((), (), s32[]{:S(2)}) async-start(), calls=%async_computation.1 | async-start | bytes 4718592 | tf_op jit(solution)/shard_map/all_gather | solution.py:55
  8.2 4.9 %collective-permute-start = (bf16[1024,2,32]{0,2,1:T(8,128)(2,1)S(1)}, bf16[1024,2,32]{0,2,1:T(8,128)(2,1)S(1)}, u32[]{:S(2)}, u32[]{:S(2)}) collective-permute-start(bf16[1024,2,32]{0,2,1:T(8,128)(2,1)S(1)} %pad_maximum_fusion.2), channel_id=1, source_target_pairs={{0,1},{1,0},{2,3},{3,2},{4,5},{5,4},{6,7},{7,6},{8,9},{9,8},{10,11... | collective-permute-start | bytes 393224 | tf_op jit(solution)/shard_map/ppermute | solution.py:10
  14.0 15.2 %collective-permute-start.1 = (bf16[1024,2,64]{0,2,1:T(8,128)(2,1)S(1)}, bf16[1024,2,64]{0,2,1:T(8,128)(2,1)S(1)}, u32[]{:S(2)}, u32[]{:S(2)}) collective-permute-start(bf16[1024,2,64]{0,2,1:T(8,128)(2,1)S(1)} %pad_maximum_fusion.1), channel_id=1, source_target_pairs={{0,2},{1,3},{2,0},{3,1},{4,6},{5,7},{6,4},{7,5},{8,10},{9,11},{10,... | collective-permute-start | bytes 786440 | tf_op jit(solution)/shard_map/ppermute | solution.py:10
  30.2 160.5 %all-gather.14.cloned.1.call-start = ((), (), s32[]{:S(2)}) async-start(), calls=%async_computation.3 | async-start | bytes 4718592 | tf_op jit(solution)/shard_map/all_gather | solution.py:50
  30.9 187.3 %all-gather.12.cloned.1.call-start = ((), (), s32[]{:S(2)}) async-start(), calls=%async_computation.2 | async-start | bytes 1179648 | tf_op jit(solution)/shard_map/all_gather | solution.py:68
  162.4 83.4 %all-gather.16.cloned.1.call-start = ((), (), s32[]{:S(2)}) async-start(), calls=%async_computation.4 | async-start | bytes 1179648 | tf_op jit(solution)/shard_map/all_gather | solution.py:69
  163.1 118.9 %all-gather.20.cloned.1.call-start = ((), (), s32[]{:S(2)}) async-start(), calls=%async_computation.6 | async-start | bytes 4718592 | tf_op jit(solution)/shard_map/all_gather | solution.py:97
  163.7 218.7 %all-gather.18.cloned.1.call-start = ((), (), s32[]{:S(2)}) async-start(), calls=%async_computation.5 | async-start | bytes 8650752 | tf_op jit(solution)/shard_map/all_gather | solution.py:94
  223.3 5.7 %copy-start = (f32[4096,512,2]{1,0,2:T(8,128)}, f32[4096,512,2]{1,0,2:T(8,128)S(1)}, u32[]{:S(2)}) copy-start(f32[4096,512,2]{1,0,2:T(8,128)S(1)} %get-tuple-element.18) | copy-start | bytes 50331652
Sparse Core Ops, SparseCore 0:
  9.8 107.2 all-gather.7
  119.0 35.0 all-gather.9
  156.0 34.6 all-gather.13
  192.3 25.8 all-gather.11
  219.9 25.7 all-gather.15
  247.5 34.5 all-gather.19
  284.6 97.6 all-gather.17
where the time goes:
time: 397 us
  waiting for transfers between devices  312 us (79%)
  matrix products  39 us (10%)
  other arithmetic  18.7 us (5%)
  between operations  13.6 us (3%)
  local copies, waits for them, and re-layouts  6.8 us (2%)
  starting transfers between devices  6.8 us (2%)
    all_gather x1, waiting for transfers between devices, per_device(): head_panel = lax.all_gather(heads, 'col', axis=1, tiled=True)  100 us
    all_gather x1, waiting for transfers between devices, per_device(): panel = lax.all_gather(hidden, 'col', axis=1, tiled=True)  86.2 us
    all_gather x1, waiting for transfers between devices, per_device(): lax.all_gather(stacked, 'row', axis=0, tiled=True)  31.8 us
    all_gather x1, waiting for transfers between devices, per_device(): lax.all_gather(wo, 'row', axis=0, tiled=True)  24.6 us
    all_gather x1, waiting for transfers between devices, per_device(): lax.all_gather(wq, 'row', axis=0, tiled=True)  23.2 us
    all_gather x1, waiting for transfers between devices, per_device(): key_piece = lax.all_gather(keys, 'row', axis=0, tiled=True)  17.7 us
    ppermute x2, waiting for transfers between devices, partner(): lax.ppermute(array, axis, [(i, i ^ 1 << distance) for i in range(lax.axis...  13.7 us
    all_gather x1, waiting for transfers between devices, per_device(): value_piece = lax.all_gather(values, 'row', axis=0, tiled=True)  12.6 us
  transfers between devices with their start and end apart: 9, of which 9 were waited for; matrix products, arithmetic and copies ran while one was open for 13% of the time, Pallas kernels for 0%

commit v1 on v0

--- a/solution.py
+++ b/solution.py
@@ -49,12 +49,25 @@
     query_part = jnp.dot(
         columns, lax.all_gather(wq, "row", axis=0, tiled=True), preferred_element_type=jnp.float32
     )
-    pair_part = jnp.einsum(
-        "ho,omr->hmr",
-        columns,
-        lax.all_gather(stacked, "row", axis=0, tiled=True),
-        preferred_element_type=jnp.float32,
+    field_out, long_array, local_part = (
+        lax.axis_size("row"),
+        lax.axis_index("row"),
+        stacked.shape[0],
     )
+    rows = [(jj, (jj + 1) % field_out) for jj in range(field_out)]
+    z_new, pair_part = (stacked, None)
+    for nth in range(field_out):
+        all_values = lax.ppermute(z_new, "row", perm=rows) if nth < field_out - 1 else None
+        k_now = jnp.einsum(
+            "ho,omr->hmr",
+            lax.dynamic_slice_in_dim(
+                columns, (long_array - nth) % field_out * local_part, z_new.shape[0], axis=1
+            ),
+            z_new,
+            preferred_element_type=jnp.float32,
+        )
+        pair_part = k_now if pair_part is None else pair_part + k_now
+        z_new = all_values
     heads_here = wq.shape[1] // HD
     kv_here = pair_part.shape[2] // HD
     per_kv = heads_here // kv_here

time: 397 us -> 361 us (0.909)
  waiting for transfers between devices: 312 us -> 245 us
  starting transfers between devices: 6.8 us -> 24.3 us
  other arithmetic: 18.7 us -> 28.3 us
    all_gather x1, waiting for transfers between devices: 86.2 us -> 33.1 us  [per_device(): panel = lax.all_gather(hidden, 'col', axis=1, tiled=True)]
    ppermute x0 -> x7, waiting for transfers between devices: none -> 37.1 us  [per_device(): lax.ppermute(z_new, 'row', perm=rows)]
    all_gather x1 -> x0, waiting for transfers between devices: 31.8 us -> none  [per_device(): lax.all_gather(stacked, 'row', axis=0, tiled=True)]
    all_gather x1, waiting for transfers between devices: 23.2 us -> 4.24 us  [per_device(): lax.all_gather(wq, 'row', axis=0, tiled=True)]
    ppermute x0 -> x7, starting transfers between devices: none -> 17.5 us  [per_device(): lax.ppermute(z_new, 'row', perm=rows)]
    convert_element_type x0 -> x1, other arithmetic: none -> 9.97 us  [per_device(): (values_in * lax.rsqrt(meansq + 1e-05) * norm_gain).astype(jnp.bfloat16)]
    unnamed x1 -> x8, matrix products: 7.02 us -> 10.7 us
  transfers between devices with their start and end apart: 9 -> 15, of which waited for: 9 -> 14; matrix products, arithmetic and copies ran while one was open for 13% -> 18% of each run, Pallas kernels for 0% -> 0%
where the time goes in v1:
time: 361 us; the launch traced here: 360 us
  waiting for transfers between devices  245 us (68%)
  matrix products  42 us (12%)
  other arithmetic  28.3 us (8%)
  starting transfers between devices  24.3 us (7%)
  between operations  13.7 us (4%)
  local copies, waits for them, and re-layouts  6.82 us (2%)
    all_gather x1, waiting for transfers between devices, per_device(): head_panel = lax.all_gather(heads, 'col', axis=1, tiled=True)  100 us
    ppermute x7, waiting for transfers between devices, per_device(): lax.ppermute(z_new, 'row', perm=rows)  37.1 us
    all_gather x1, waiting for transfers between devices, per_device(): panel = lax.all_gather(hidden, 'col', axis=1, tiled=True)  33.1 us
    all_gather x1, waiting for transfers between devices, per_device(): lax.all_gather(wo, 'row', axis=0, tiled=True)  24.6 us
    all_gather x1, waiting for transfers between devices, per_device(): key_piece = lax.all_gather(keys, 'row', axis=0, tiled=True)  18.5 us
    ppermute x7, starting transfers between devices, per_device(): lax.ppermute(z_new, 'row', perm=rows)  17.5 us
    ppermute x2, waiting for transfers between devices, partner(): lax.ppermute(array, axis, [(i, i ^ 1 << distance) for i in range(lax.axis...  13.7 us
    all_gather x1, waiting for transfers between devices, per_device(): value_piece = lax.all_gather(values, 'row', axis=0, tiled=True)  12.6 us
  transfers between devices with their start and end apart: 15, of which 14 were waited for; matrix products, arithmetic and copies ran while one was open for 18% of the time, Pallas kernels for 0%

profile of v1, /device:TPU:1, one launch (start us, length us, event | category | flops | bytes accessed | tf_op | source)
XLA Modules:
  0.0 360.3 jit_solution(18051121846124449026)
XLA Ops:
  6.5 0.0 all-gather.7.cloned.1.call-start
  6.5 0.7 all-gather.7.cloned.1.call-update
  7.3 0.0 all-gather.11.cloned.1.call-start
  7.3 0.9 pad_maximum_fusion.2
  8.2 2.6 collective-permute-start
  10.7 2.4 collective-permute-done
  13.1 0.9 broadcast_select_fusion.3
  14.0 3.8 %collective-permute-start.1 = (bf16[1024,2,64]{0,2,1:T(8,128)(2,1)S(1)}, bf16[1024,2,64]{0,2,1:T(8,128)(2,1)S(1)}, u32[]{:S(2)}, u32[]{:S(2)}) collective-permute-start(bf16[1024,2,64]{0,2,1:T(8,128)(2,1)S(1)} %pad_maximum_fusion.1), channel_id=1, source_target_pairs={{0,2},{1,3},{2,0},{3,1},{4,6},{5,7},{6,4},{7,5},{8,10},{9,11},{10,... | collective-permute-start | bytes 786440 | tf_op jit(solution)/shard_map/ppermute | solution.py:10
  17.9 11.3 %collective-permute-done.1 = bf16[1024,2,64]{0,2,1:T(8,128)(2,1)S(1)} collective-permute-done((bf16[1024,2,64]{0,2,1:T(8,128)(2,1)S(1)}, bf16[1024,2,64]{0,2,1:T(8,128)(2,1)S(1)}, u32[]{:S(2)}, u32[]{:S(2)}) %collective-permute-start.1) | collective-permute-done | bytes 262176 | tf_op jit(solution)/shard_map/ppermute | solution.py:10
  29.2 0.1 broadcast_select_fusion.1
  29.4 2.8 collective-permute-start.2
  32.1 6.1 %collective-permute-done.2 = bf16[1024,2,128]{0,2,1:T(8,128)(2,1)S(1)} collective-permute-done((bf16[1024,2,128]{0,2,1:T(8,128)(2,1)S(1)}, bf16[1024,2,128]{0,2,1:T(8,128)(2,1)S(1)}, u32[]{:S(2)}, u32[]{:S(2)}) %collective-permute-start.2) | collective-permute-done | bytes 524320 | tf_op jit(solution)/shard_map/ppermute | solution.py:60
  38.2 2.5 collective-permute-start.3
  40.7 6.1 %collective-permute-done.3 = bf16[1024,2,128]{0,2,1:T(8,128)(2,1)S(1)} collective-permute-done((bf16[1024,2,128]{0,2,1:T(8,128)(2,1)S(1)}, bf16[1024,2,128]{0,2,1:T(8,128)(2,1)S(1)}, u32[]{:S(2)}, u32[]{:S(2)}) %collective-permute-start.3) | collective-permute-done | bytes 524320 | tf_op jit(solution)/shard_map/ppermute | solution.py:60
  46.8 2.5 collective-permute-start.4
  49.3 0.0 all-gather.11.cloned.1.call-update
  49.3 0.0 all-gather.9.cloned.1.call-start
  49.4 6.1 %collective-permute-done.4 = bf16[1024,2,128]{0,2,1:T(8,128)(2,1)S(1)} collective-permute-done((bf16[1024,2,128]{0,2,1:T(8,128)(2,1)S(1)}, bf16[1024,2,128]{0,2,1:T(8,128)(2,1)S(1)}, u32[]{:S(2)}, u32[]{:S(2)}) %collective-permute-start.4) | collective-permute-done | bytes 524320 | tf_op jit(solution)/shard_map/ppermute | solution.py:60
  55.4 2.5 collective-permute-start.5
  57.9 6.1 %collective-permute-done.5 = bf16[1024,2,128]{0,2,1:T(8,128)(2,1)S(1)} collective-permute-done((bf16[1024,2,128]{0,2,1:T(8,128)(2,1)S(1)}, bf16[1024,2,128]{0,2,1:T(8,128)(2,1)S(1)}, u32[]{:S(2)}, u32[]{:S(2)}) %collective-permute-start.5) | collective-permute-done | bytes 524320 | tf_op jit(solution)/shard_map/ppermute | solution.py:60
  64.1 2.5 collective-permute-start.6
  66.5 6.1 %collective-permute-done.6 = bf16[1024,2,128]{0,2,1:T(8,128)(2,1)} collective-permute-done((bf16[1024,2,128]{0,2,1:T(8,128)(2,1)S(1)}, bf16[1024,2,128]{0,2,1:T(8,128)(2,1)}, u32[]{:S(2)}, u32[]{:S(2)}) %collective-permute-start.6) | collective-permute-done | bytes 524320 | tf_op jit(solution)/shard_map/ppermute | solution.py:60
  72.7 2.6 collective-permute-start.7
  75.3 6.6 %collective-permute-done.7 = bf16[1024,2,128]{0,2,1:T(8,128)(2,1)S(1)} collective-permute-done((bf16[1024,2,128]{0,2,1:T(8,128)(2,1)}, bf16[1024,2,128]{0,2,1:T(8,128)(2,1)S(1)}, u32[]{:S(2)}, u32[]{:S(2)}) %collective-permute-start.7) | collective-permute-done | bytes 524320 | tf_op jit(solution)/shard_map/ppermute | solution.py:60
  81.8 2.3 collective-permute-start.8
  84.1 33.1 %all-gather.7.cloned.1.call-done = bf16[512,8192]{1,0:T(8,128)(2,1)} async-done(((bf16[512,256]{1,0:T(8,128)(2,1)}), bf16[512,8192]{1,0:T(8,128)(2,1)}) %all-gather.7.cloned.1.call-update) | async-done | bytes 8388624 | tf_op jit(solution)/shard_map/all_gather | solution.py:36
  117.1 5.1 %fusion = f32[512]{0:T(512)S(1)} fusion(bf16[512,8192]{1,0:T(8,128)(2,1)} %all-gather.7.cloned.1.call-done), kind=kLoop, calls=%fused_computation.2 | loop fusion | flops 12582400 | bytes 8390656 | tf_op jit(solution)/shard_map/reduce_sum | solution.py:38
  122.2 10.0 %fusion.2 = bf16[512,8192]{1,0:T(8,128)(2,1)} fusion(bf16[512,8192]{1,0:T(8,128)(2,1)} %all-gather.7.cloned.1.call-done, f32[8192]{0:T(1024)S(1)} %copy-done.2, f32[512]{0:T(512)S(1)} %add_rsqrt_fusion), kind=kLoop, calls=%fused_computation.4 | loop fusion | flops 16777216 | bytes 16812032 | tf_op jit(solution)/shard_map/convert_element_type | solution.py:39
  132.2 1.9 fusion.19
  134.1 2.2 fusion.21
  136.4 1.8 fusion.17
  138.2 1.8 fusion.23
  140.0 0.5 fusion.15
  140.5 0.5 fusion.25
  141.0 0.0 collective-permute-done.8
  141.0 1.5 fusion.13
  142.5 0.5 fusion.27
  143.0 0.5 add_add_fusion
  143.5 0.6 fusion.47
  144.1 0.7 pad_maximum_fusion.3
  144.7 0.0 all-gather.9.cloned.1.call-update
  144.7 0.0 all-gather.13.cloned.1.call-start
  144.8 0.7 slice.34
  145.5 0.0 all-gather.13.cloned.1.call-update
  145.5 0.0 all-gather.17.cloned.1.call-start
  145.5 0.5 all-gather.17.cloned.1.call-update
  146.1 0.2 all-gather.15.cloned.1.call-start
  146.3 1.8 multiply_cosine_fusion
  148.1 1.7 iota_compare_fusion
  149.9 4.2 %all-gather.11.cloned.1.call-done = bf16[8192,256]{1,0:T(8,128)(2,1)} async-done(((bf16[1024,256]{1,0:T(8,128)(2,1)}), bf16[8192,256]{1,0:T(8,128)(2,1)}) %all-gather.11.cloned.1.call-update) | async-done | bytes 4194320 | tf_op jit(solution)/shard_map/all_gather | solution.py:50
  154.1 6.9 %fusion.63 = f32[512,256]{0,1:T(8,128)S(1)} fusion(bf16[512,8192]{1,0:T(8,128)(2,1)} %fusion.2, bf16[8192,256]{1,0:T(8,128)(2,1)} %all-gather.11.cloned.1.call-done), kind=kOutput, calls=%fused_computation.80 | convolution fusion | flops 2147483648 | bytes 13107200 | tf_op jit(solution)/shard_map/dot_general | solution.py:49
  161.1 0.2 copy.14
  161.3 0.2 copy.15
  161.5 1.9 subtract_convert_fusion
  163.4 18.5 %all-gather.9.cloned.1.call-done = bf16[4096,1,128]{0,2,1:T(8,128)(2,1)} async-done(((bf16[512,1,128]{0,2,1:T(8,128)(2,1)}), bf16[4096,1,128]{0,2,1:T(8,128)(2,1)}) %all-gather.9.cloned.1.call-update) | async-done | bytes 1048592 | tf_op jit(solution)/shard_map/all_gather | solution.py:81
  181.9 5.1 %fusion.5 = (f32[2,512]{1,0:T(2,128)S(1)}, f32[4096,512,2]{1,0,2:T(8,128)S(1)}) fusion(pred[512,4096]{0,1:T(8,128)(4,1)S(1)} %iota_compare_fusion, bf16[512,2,64]{2,0,1:T(8,128)(2,1)} %get-tuple-element.6, bf16[512,2,64]{2,0,1:T(8,128)(2,1)S(1)} %get-tuple-element.5, bf16[4096,1,128]{0,2,1:T(8,128)(2,1)} %all-gather.9.cloned.1.call-done), kind=kOutput, calls=%fused_computation.9 | convolution fusion | flops 1086848000 | bytes 20189184 | tf_op jit(solution)/shard_map/tagd,nad->agtn/dot_general | solution.py:85
  187.0 5.7 %copy-done.1 = f32[4096,512,2]{1,0,2:T(8,128)} copy-done((f32[4096,512,2]{1,0,2:T(8,128)}, f32[4096,512,2]{1,0,2:T(8,128)S(1)}, u32[]{:S(2)}) %copy-start.1) | copy-done | bytes 16777240
  192.7 4.2 %fusion.3 = f32[2,512]{1,0:T(2,128)S(1)} fusion(f32[4096,512,2]{1,0,2:T(8,128)S(1)} %get-tuple-element.18, f32[2,512]{1,0:T(2,128)S(1)} %broadcast_maximum_fusion, pred[512,4096]{0,1:T(8,128)(4,1)S(1)} %iota_compare_fusion), kind=kLoop, calls=%fused_computation.7 | loop fusion | flops 16776192 | bytes 18882560 | tf_op jit(solution)/shard_map/reduce_sum | solution.py:92
  196.8 12.6 %all-gather.13.cloned.1.call-done = bf16[4096,1,128]{0,2,1:T(8,128)(2,1)} async-done(((bf16[512,1,128]{0,2,1:T(8,128)(2,1)}), bf16[4096,1,128]{0,2,1:T(8,128)(2,1)}) %all-gather.13.cloned.1.call-update) | async-done | bytes 1048592 | tf_op jit(solution)/shard_map/all_gather | solution.py:82
  209.4 11.7 %fusion.34 = bf16[2,512,128]{1,2,0:T(8,128)(2,1)} fusion(f32[4096,512,2]{1,0,2:T(8,128)} %copy-done.1, f32[2,512]{1,0:T(2,128)S(1)} %broadcast_maximum_fusion, pred[512,4096]{0,1:T(8,128)(4,1)S(1)} %iota_compare_fusion, bf16[4096,1,128]{0,2,1:T(8,128)(2,1)} %all-gather.13.cloned.1.call-done, f32[2,512]{1,0:T(2,128)S(1)} %fusion.3), kind=kOutput, calls=%fused_computation.35 | convolution fusion | flops 1090781184 | bytes 20193280 | tf_op jit(solution)/shard_map/agtn,nad->agtd/dot_general | solution.py:93
  221.0 0.0 all-gather.15.cloned.1.call-update
  221.1 24.6 %all-gather.17.cloned.1.call-done = bf16[8192,256]{1,0:T(8,128)(2,1)} async-done(((bf16[1024,256]{1,0:T(8,128)(2,1)}), bf16[8192,256]{1,0:T(8,128)(2,1)}) %all-gather.17.cloned.1.call-update) | async-done | bytes 4194320 | tf_op jit(solution)/shard_map/all_gather | solution.py:110
  245.7 100.2 %all-gather.15.cloned.1.call-done = bf16[512,8192]{0,1:T(8,128)(2,1)} async-done(((bf16[512,256]{0,1:T(8,128)(2,1)}), bf16[512,8192]{0,1:T(8,128)(2,1)}) %all-gather.15.cloned.1.call-update) | async-done | bytes 8388624 | tf_op jit(solution)/shard_map/all_gather | solution.py:107
  345.8 7.7 %convolution_convert_fusion = bf16[512,256]{1,0:T(8,128)(2,1)} fusion(bf16[512,8192]{0,1:T(8,128)(2,1)} %all-gather.15.cloned.1.call-done, bf16[8192,256]{1,0:T(8,128)(2,1)} %all-gather.17.cloned.1.call-done), kind=kOutput, calls=%fused_computation.14 | convolution fusion | flops 2147614720 | bytes 12845056 | tf_op jit(solution)/shard_map/dot_general | solution.py:109
  (13 shorter events, 0.1 us)
Async XLA Ops:
  6.5 115.7 %copy-start.2 = (f32[8192]{0:T(1024)S(1)}, f32[8192]{0:T(1024)}, u32[]{:S(2)}) copy-start(f32[8192]{0:T(1024)} %param.7) | copy-start | bytes 98308
  6.5 110.6 %all-gather.7.cloned.1.call-start = ((), (), s32[]{:S(2)}) async-start(), calls=%async_computation | async-start | bytes 8650752 | tf_op jit(solution)/shard_map/all_gather | solution.py:36
  7.3 146.8 %all-gather.11.cloned.1.call-start = ((), (), s32[]{:S(2)}) async-start(), calls=%async_computation.2 | async-start | bytes 4718592 | tf_op jit(solution)/shard_map/all_gather | solution.py:50
  8.2 4.9 %collective-permute-start = (bf16[1024,2,32]{0,2,1:T(8,128)(2,1)S(1)}, bf16[1024,2,32]{0,2,1:T(8,128)(2,1)S(1)}, u32[]{:S(2)}, u32[]{:S(2)}) collective-permute-start(bf16[1024,2,32]{0,2,1:T(8,128)(2,1)S(1)} %pad_maximum_fusion.2), channel_id=1, source_target_pairs={{0,1},{1,0},{2,3},{3,2},{4,5},{5,4},{6,7},{7,6},{8,9},{9,8},{10,11... | collective-permute-start | bytes 393224 | tf_op jit(solution)/shard_map/ppermute | solution.py:10
  14.0 15.2 %collective-permute-start.1 = (bf16[1024,2,64]{0,2,1:T(8,128)(2,1)S(1)}, bf16[1024,2,64]{0,2,1:T(8,128)(2,1)S(1)}, u32[]{:S(2)}, u32[]{:S(2)}) collective-permute-start(bf16[1024,2,64]{0,2,1:T(8,128)(2,1)S(1)} %pad_maximum_fusion.1), channel_id=1, source_target_pairs={{0,2},{1,3},{2,0},{3,1},{4,6},{5,7},{6,4},{7,5},{8,10},{9,11},{10,... | collective-permute-start | bytes 786440 | tf_op jit(solution)/shard_map/ppermute | solution.py:10
  29.4 8.9 %collective-permute-start.2 = (bf16[1024,2,128]{0,2,1:T(8,128)(2,1)S(1)}, bf16[1024,2,128]{0,2,1:T(8,128)(2,1)S(1)}, u32[]{:S(2)}, u32[]{:S(2)}) collective-permute-start(bf16[1024,2,128]{0,2,1:T(8,128)(2,1)S(1)} %pad_maximum_fusion), channel_id=1, source_target_pairs={{0,32},{32,64},{64,96},{96,128},{128,160},{160,192},{192,224},{224... | collective-permute-start | bytes 1572872 | tf_op jit(solution)/shard_map/ppermute | solution.py:60
  38.2 8.6 %collective-permute-start.3 = (bf16[1024,2,128]{0,2,1:T(8,128)(2,1)S(1)}, bf16[1024,2,128]{0,2,1:T(8,128)(2,1)S(1)}, u32[]{:S(2)}, u32[]{:S(2)}) collective-permute-start(bf16[1024,2,128]{0,2,1:T(8,128)(2,1)S(1)} %collective-permute-done.2), channel_id=1, source_target_pairs={{0,32},{32,64},{64,96},{96,128},{128,160},{160,192},{192,224},{224... | collective-permute-start | bytes 1572872 | tf_op jit(solution)/shard_map/ppermute | solution.py:60
  46.8 8.6 %collective-permute-start.4 = (bf16[1024,2,128]{0,2,1:T(8,128)(2,1)S(1)}, bf16[1024,2,128]{0,2,1:T(8,128)(2,1)S(1)}, u32[]{:S(2)}, u32[]{:S(2)}) collective-permute-start(bf16[1024,2,128]{0,2,1:T(8,128)(2,1)S(1)} %collective-permute-done.3), channel_id=1, source_target_pairs={{0,32},{32,64},{64,96},{96,128},{128,160},{160,192},{192,224},{224... | collective-permute-start | bytes 1572872 | tf_op jit(solution)/shard_map/ppermute | solution.py:60
  49.3 132.5 %all-gather.9.cloned.1.call-start = ((), (), s32[]{:S(2)}) async-start(), calls=%async_computation.1 | async-start | bytes 1179648 | tf_op jit(solution)/shard_map/all_gather | solution.py:81
  55.4 8.6 %collective-permute-start.5 = (bf16[1024,2,128]{0,2,1:T(8,128)(2,1)S(1)}, bf16[1024,2,128]{0,2,1:T(8,128)(2,1)S(1)}, u32[]{:S(2)}, u32[]{:S(2)}) collective-permute-start(bf16[1024,2,128]{0,2,1:T(8,128)(2,1)S(1)} %collective-permute-done.4), channel_id=1, source_target_pairs={{0,32},{32,64},{64,96},{96,128},{128,160},{160,192},{192,224},{224... | collective-permute-start | bytes 1572872 | tf_op jit(solution)/shard_map/ppermute | solution.py:60
  64.1 8.6 %collective-permute-start.6 = (bf16[1024,2,128]{0,2,1:T(8,128)(2,1)S(1)}, bf16[1024,2,128]{0,2,1:T(8,128)(2,1)}, u32[]{:S(2)}, u32[]{:S(2)}) collective-permute-start(bf16[1024,2,128]{0,2,1:T(8,128)(2,1)S(1)} %collective-permute-done.5), channel_id=1, source_target_pairs={{0,32},{32,64},{64,96},{96,128},{128,160},{160,192},{192,224},{224... | collective-permute-start | bytes 1572872 | tf_op jit(solution)/shard_map/ppermute | solution.py:60
  72.7 9.1 %collective-permute-start.7 = (bf16[1024,2,128]{0,2,1:T(8,128)(2,1)}, bf16[1024,2,128]{0,2,1:T(8,128)(2,1)S(1)}, u32[]{:S(2)}, u32[]{:S(2)}) collective-permute-start(bf16[1024,2,128]{0,2,1:T(8,128)(2,1)} %collective-permute-done.6), channel_id=1, source_target_pairs={{0,32},{32,64},{64,96},{96,128},{128,160},{160,192},{192,224},{224... | collective-permute-start | bytes 1572872 | tf_op jit(solution)/shard_map/ppermute | solution.py:60
  81.8 59.1 %collective-permute-start.8 = (bf16[1024,2,128]{0,2,1:T(8,128)(2,1)S(1)}, bf16[1024,2,128]{0,2,1:T(8,128)(2,1)}, u32[]{:S(2)}, u32[]{:S(2)}) collective-permute-start(bf16[1024,2,128]{0,2,1:T(8,128)(2,1)S(1)} %collective-permute-done.7), channel_id=1, source_target_pairs={{0,32},{32,64},{64,96},{96,128},{128,160},{160,192},{192,224},{224... | collective-permute-start | bytes 1572872 | tf_op jit(solution)/shard_map/ppermute | solution.py:60
  132.2 7.8 %copy-start = (bf16[512,8192]{1,0:T(8,128)(2,1)S(1)}, bf16[512,8192]{1,0:T(8,128)(2,1)}, u32[]{:S(2)}) copy-start(bf16[512,8192]{1,0:T(8,128)(2,1)} %fusion.2) | copy-start | bytes 25165828
  144.7 64.7 %all-gather.13.cloned.1.call-start = ((), (), s32[]{:S(2)}) async-start(), calls=%async_computation.3 | async-start | bytes 1179648 | tf_op jit(solution)/shard_map/all_gather | solution.py:82
  145.5 100.2 %all-gather.17.cloned.1.call-start = ((), (), s32[]{:S(2)}) async-start(), calls=%async_computation.5 | async-start | bytes 4718592 | tf_op jit(solution)/shard_map/all_gather | solution.py:110
  146.1 199.7 %all-gather.15.cloned.1.call-start = ((), (), s32[]{:S(2)}) async-start(), calls=%async_computation.4 | async-start | bytes 8650752 | tf_op jit(solution)/shard_map/all_gather | solution.py:107
  186.9 5.7 %copy-start.1 = (f32[4096,512,2]{1,0,2:T(8,128)}, f32[4096,512,2]{1,0,2:T(8,128)S(1)}, u32[]{:S(2)}) copy-start(f32[4096,512,2]{1,0,2:T(8,128)S(1)} %get-tuple-element.18) | copy-start | bytes 50331652
Sparse Core Ops, SparseCore 0:
  9.8 107.2 all-gather.6
  119.0 35.0 all-gather.10
  155.9 25.8 all-gather.8
  183.6 25.7 all-gather.12
  211.1 34.5 all-gather.16
  248.1 97.6 all-gather.14
